TPU v7x, 512 devices: a whole 4x8x8 slice. The times are simulated.
512 devices in a mesh: tok: 16 (over z, core), voc: 32 (over y, x).
Axes of the slice: x: 4, y: 8, z: 8, core: 2. Of those that a mesh axis runs over, the one named last changes fastest.
Arguments:
- hidden: bfloat16 [256, 2304], P('tok', 'voc'), may hold values from -18 to 18
- head: bfloat16 [2304, 131072], P(None, ('tok', 'voc')), as said below
- targets: int32 [256], replicated, may hold values from 0 to 131071
- probe_hidden: bfloat16 [256, 2304], P('tok', 'voc'), may hold values from -6 to 6
- probe_head: bfloat16 [2304, 131072], P(None, ('tok', 'voc')), may hold values from -0.5 to 0.5
Outputs:
- head_out: float32 [2304, 131072], P(None, ('tok', 'voc'))
- hidden_out: float32 [256, 2304], P('tok', 'voc')
Inputs may be any that keep to these rules, and one draw needn't show every extreme that they name: `head`: entries lie within 66 / sqrt(2304) in magnitude.
All inputs are finite; a program needn't handle non-finite values.
Results may differ from a plain program's by a relative error of at most 0.0075.
Values may be sent and summed in bfloat16 or wider, within the bound.
A program may use at most 64 MiB of HBM per device.

v0:
```python
import jax
import jax.numpy as jnp
from jax import lax
import numpy as np
from jax.sharding import Mesh, PartitionSpec as P

softcap_value = 30.0
zloss_weight = 0.0001


def local(hidden, head, targets, probe_hidden, probe_head):
    voc_count = lax.axis_size("vy") * lax.axis_size("vx")
    vocab_width = head.shape[1]
    rows_here = hidden.shape[0]
    stacked = jnp.stack([hidden, probe_hidden])
    copies = jnp.broadcast_to(stacked[None], (voc_count,) + stacked.shape)
    blocks = lax.all_to_all(copies, ("vy", "vx"), 0, 0, tiled=True)
    features = blocks.transpose(1, 2, 0, 3).reshape(2, rows_here, voc_count * stacked.shape[2])
    gathered = lax.all_gather(features, "tok", axis=1, tiled=True)
    row_hidden = gathered[0]
    row_probe = gathered[1]
    logits = jnp.dot(row_hidden, head, preferred_element_type=jnp.float32)
    tangent = jnp.dot(row_probe, head, preferred_element_type=jnp.float32) + jnp.dot(
        row_hidden, probe_head, preferred_element_type=jnp.float32
    )
    capped = jnp.tanh(logits / softcap_value)
    cap_slope = 1.0 - capped * capped
    exponent = jnp.exp(softcap_value * capped)
    cap_tangent = cap_slope * tangent
    slope_tan = -2.0 / softcap_value * capped * cap_slope * tangent
    voc_index = lax.axis_index("vy") * lax.axis_size("vx") + lax.axis_index("vx")
    offset = (lax.axis_index("tok") * voc_count + voc_index) * vocab_width
    columns = offset + lax.iota(jnp.int32, vocab_width)
    onehot = (targets[:, None] == columns[None, :]).astype(jnp.float32)
    weighted_slope = exponent * cap_slope
    weighted_tan = exponent * (cap_slope * cap_tangent + slope_tan)
    hi = lax.Precision.HIGH
    by_probe = lax.dot_general(
        jnp.stack([weighted_slope, onehot * cap_slope]),
        probe_head.astype(jnp.float32),
        (((2,), (1,)), ((), ())),
        precision=hi,
        preferred_element_type=jnp.float32,
    )
    by_head = lax.dot_general(
        jnp.stack([weighted_tan, weighted_slope, onehot * slope_tan]),
        head.astype(jnp.float32),
        (((2,), (1,)), ((), ())),
        precision=hi,
        preferred_element_type=jnp.float32,
    )
    partials = jnp.stack([by_probe[0] + by_head[0], by_head[1], by_probe[1] + by_head[2]])
    local_stats = jnp.stack([jnp.sum(exponent, axis=1), jnp.sum(exponent * cap_tangent, axis=1)])
    partials, local_stats = lax.optimization_barrier((partials, local_stats))
    summed = lax.psum_scatter(partials, "tok", scatter_dimension=1, tiled=True)
    stats = lax.psum(lax.psum(lax.psum(local_stats, "tok"), "vy"), "vx")
    kinds, rows, width = summed.shape
    blocks = summed.reshape(kinds, rows, voc_count, width // voc_count).transpose(2, 0, 1, 3)
    reduced = jnp.sum(lax.all_to_all(blocks, ("vy", "vx"), 0, 0, tiled=True), axis=0)
    row_total = stats[0]
    probability = exponent / row_total[:, None]
    mean_tangent = stats[1] / row_total
    factor = 1.0 + 2.0 * zloss_weight * jnp.log(row_total)
    grad_cap = factor[:, None] * probability - onehot
    grad_tan = probability * (
        factor[:, None] * (cap_tangent - mean_tangent[:, None])
        + 2.0 * zloss_weight * mean_tangent[:, None]
    )
    dlogit = (grad_cap * cap_slope).astype(jnp.bfloat16)
    dlogit_tan = (grad_tan * cap_slope + grad_cap * slope_tan).astype(jnp.bfloat16)
    head_out = jnp.einsum(
        "krd,krv->dv", gathered, jnp.stack([dlogit_tan, dlogit]), preferred_element_type=jnp.float32
    )
    first_row = lax.axis_index("tok") * rows_here
    own_total = lax.dynamic_slice_in_dim(row_total, first_row, rows_here)
    own_mean = lax.dynamic_slice_in_dim(mean_tangent, first_row, rows_here)
    own_factor = lax.dynamic_slice_in_dim(factor, first_row, rows_here)
    scale_main = (own_factor / own_total)[:, None]
    scale_mean = ((2.0 * zloss_weight - own_factor) * own_mean / own_total)[:, None]
    hidden_out = scale_main * reduced[0] + scale_mean * reduced[1] - reduced[2]
    return (head_out, hidden_out)


def solution(mesh):
    tok_size, voc_size = mesh.devices.shape
    x_size = 4 if voc_size % 4 == 0 else 1
    split = Mesh(
        np.asarray(mesh.devices).reshape(tok_size, voc_size // x_size, x_size), ("tok", "vy", "vx")
    )
    voc = ("vy", "vx")
    return jax.shard_map(
        local,
        mesh=split,
        in_specs=(
            P("tok", voc),
            P(None, ("tok",) + voc),
            P(),
            P("tok", voc),
            P(None, ("tok",) + voc),
        ),
        out_specs=(P(None, ("tok",) + voc), P("tok", voc)),
        check_vma=False,
    )
```

profile of v0, /device:TPU:2, one launch (start us, length us, event | category | flops | bytes accessed | tf_op | source)
XLA Modules:
  0.0 204.7 jit_solution(5712569975829166852)
XLA Ops:
  7.2 0.0 copy-start
  7.2 0.0 all-gather.2.cloned.1.call-start
  7.2 0.8 pad_maximum_fusion.1
  8.1 21.4 %all_to_all.10 = bf16[32,2,16,72]{3,2,1,0:T(8,128)(2,1)S(1)} all-to-all(bf16[32,2,16,72]{3,2,1,0:T(8,128)(2,1)S(1)} %broadcast_in_dim.2), channel_id=1, replica_groups=mesh['tok'=16,'vy'=8,'vx'=4] {'vy','vx'}, dimensions={0} | all-to-all | bytes 294912 | tf_op jit(solution)/shard_map/all_to_all | solution.py:17
  29.5 0.1 copy.10
  29.6 1.0 reshape.44
  30.6 0.0 all-gather.2.cloned.1.call-update
  30.6 0.0 reduce-scatter.2.cloned.1.call-start
  30.7 43.2 %all-gather.2.cloned.1.call-done = bf16[2,256,2304]{2,1,0:T(8,128)(2,1)} async-done(((bf16[2,16,2304]{2,1,0:T(8,128)(2,1)}), bf16[2,256,2304]{2,1,0:T(8,128)(2,1)}) %all-gather.2.cloned.1.call-update) | async-done | bytes 2359312 | tf_op jit(solution)/shard_map/all_gather | solution.py:19
  73.9 2.0 fusion.6
  75.9 0.0 copy-done.1
  75.9 0.6 fusion.7
  76.5 0.6 fusion.5
  77.2 0.2 fusion.24
  77.4 2.7 %fusion.3 = f32[2,256,2304]{2,1,0:T(8,128)S(1)} fusion(bf16[2304,256]{1,0:T(8,128)(2,1)S(1)} %copy-done.4, f32[1,256,256]{1,2,0:T(8,128)S(1)} %get-tuple-element.17, f32[1,256,256]{1,2,0:T(8,128)S(1)} %get-tuple-element.18), kind=kOutput, calls=%fused_computation.9 | convolution fusion | flops 1812070400 | bytes 6422528 | tf_op jit(solution)/shard_map/dot_general | solution.py:38
  80.1 4.0 %fusion.1 = f32[3,256,2304]{2,1,0:T(8,128)S(1)} fusion(bf16[2304,256]{1,0:T(8,128)(2,1)S(1)} %copy-done, f32[1,256,256]{1,2,0:T(8,128)S(1)} %get-tuple-element.14, f32[1,256,256]{1,2,0:T(8,128)S(1)} %get-tuple-element.18, f32[1,256,256]{1,2,0:T(8,128)S(1)} %get-tuple-element.13), kind=kOutput, calls=%fused_computation.7 | convolution fusion | flops 2718302208 | bytes 9043968 | tf_op jit(solution)/shard_map/dot_general | solution.py:45
  84.1 2.1 %slice_add_fusion.1 = (f32[1,256,2304]{2,1,0:T(8,128)S(1)}, f32[1,256,2304]{2,1,0:T(8,128)S(1)}, f32[1,256,2304]{2,1,0:T(8,128)}) fusion(f32[3,256,2304]{2,1,0:T(8,128)S(1)} %fusion.1, f32[2,256,2304]{2,1,0:T(8,128)S(1)} %fusion.3), kind=kLoop, calls=%fused_computation.3 | loop fusion | flops 1179648 | bytes 18874368 | tf_op jit(solution)/shard_map/add | solution.py:52
  86.2 5.1 %pad_maximum_fusion = f32[3,256,2304]{2,1,0:T(8,128)} fusion(f32[1,256,2304]{2,1,0:T(8,128)S(1)} %get-tuple-element.11, f32[1,256,2304]{2,1,0:T(8,128)} %get-tuple-element.12, f32[1,256,2304]{2,1,0:T(8,128)S(1)} %get-tuple-element.10), kind=kLoop, calls=%fused_computation | loop fusion | flops 3538944 | bytes 14155776 | tf_op jit(solution)/shard_map/stack | solution.py:52
  91.3 0.0 reduce-scatter.2.cloned.1.call-update
  91.4 25.1 %psum.21 = f32[2,256]{1,0:T(2,128)S(1)} all-reduce(f32[2,256]{1,0:T(2,128)S(1)} %pad_maximum_fusion.2), channel_id=1, replica_groups=mesh['tok'=16,'vy'=8,'vx'=4] {'tok'}, use_global_device_ids=true, to_apply=%region_2.0 | all-reduce | flops 512 | bytes 4096 | tf_op jit(solution)/shard_map/psum | solution.py:56
  116.5 16.9 %psum.22 = f32[2,256]{1,0:T(2,128)S(1)} all-reduce(f32[2,256]{1,0:T(2,128)S(1)} %psum.21), channel_id=1, replica_groups=mesh['tok'=16,'vy'=8,'vx'=4] {'vy'}, use_global_device_ids=true, to_apply=%region_3.0 | all-reduce | flops 512 | bytes 4096 | tf_op jit(solution)/shard_map/psum | solution.py:56
  133.4 8.8 %psum.23 = f32[2,256]{1,0:T(2,128)S(1)} all-reduce(f32[2,256]{1,0:T(2,128)S(1)} %psum.22), channel_id=1, replica_groups=mesh['tok'=16,'vy'=8,'vx'=4] {'vx'}, use_global_device_ids=true, to_apply=%region_4.0 | all-reduce | flops 512 | bytes 4096 | tf_op jit(solution)/shard_map/psum | solution.py:56
  142.2 19.3 %reduce-scatter.2.cloned.1.call-done = f32[3,16,2304]{2,1,0:T(8,128)} async-done(((f32[3,256,2304]{2,1,0:T(8,128)}), f32[3,16,2304]{2,1,0:T(8,128)}) %reduce-scatter.2.cloned.1.call-update) | async-done | bytes 442384 | tf_op jit(solution)/shard_map/reduce_scatter | solution.py:55
  161.5 2.7 %reshape.45 = f32[3,16,32,72]{3,2,1,0:T(8,128)} reshape(f32[3,16,2304]{2,1,0:T(8,128)} %reduce-scatter.2.cloned.1.call-done) | data formatting | bytes 884736 | tf_op jit(solution)/shard_map/reshape | solution.py:58
  164.2 2.5 %copy.19 = f32[3,16,32,72]{3,1,0,2:T(8,128)} copy(f32[3,16,32,72]{3,2,1,0:T(8,128)} %reshape.45) | data formatting | bytes 884736 | tf_op jit(solution)/shard_map/reshape | solution.py:58
  166.7 9.8 %all-to-all-start.1 = ((f32[32,3,16,72]{3,2,1,0:T(8,128)}), f32[32,3,16,72]{3,2,1,0:T(8,128)}, u32[]{:S(2)}, u32[]{:S(2)}) async-start(f32[32,3,16,72]{3,2,1,0:T(8,128)} %bitcast.66), calls=%async_computation.2 | async-start | bytes 1572864 | tf_op jit(solution)/shard_map/all_to_all | solution.py:59
  176.5 0.6 bitcast_divide_fusion.1
  177.1 1.2 fusion.26
  178.4 2.2 %convolution_bitcast_fusion = f32[2304,256]{1,0:T(8,128)} fusion(bf16[2,256,2304]{2,1,0:T(8,128)(2,1)S(1)} %copy-done.2, bf16[1,256,256]{1,2,0:T(8,128)(2,1)S(1)} %get-tuple-element.16, bf16[1,256,256]{1,2,0:T(8,128)(2,1)S(1)} %get-tuple-element.15), kind=kOutput, calls=%fused_computation.1 | convolution fusion | flops 604110848 | bytes 4980736 | tf_op jit(solution)/shard_map/krd,krv->dv/dot_general | solution.py:71
  180.6 15.3 %all-to-all-done.1 = f32[32,3,16,72]{3,2,1,0:T(8,128)} async-done(((f32[32,3,16,72]{3,2,1,0:T(8,128)}), f32[32,3,16,72]{3,2,1,0:T(8,128)}, u32[]{:S(2)}, u32[]{:S(2)}) %all-to-all-start.1) | async-done | bytes 442400 | tf_op jit(solution)/shard_map/all_to_all | solution.py:59
  196.0 1.2 reduce_sum.29
  197.2 0.7 fusion.27
  (19 shorter events, 0.1 us)
Async XLA Ops:
  7.2 66.7 %copy-start = (bf16[2304,256]{1,0:T(8,128)(2,1)S(1)}, bf16[2304,256]{1,0:T(8,128)(2,1)}, u32[]{:S(2)}) copy-start(bf16[2304,256]{1,0:T(8,128)(2,1)} %param.6) | copy-start | bytes 3538948
  7.2 66.7 %all-gather.2.cloned.1.call-start = ((), (), s32[]{:S(2)}) async-start(), calls=%async_computation.3 | async-start | bytes 2506752 | tf_op jit(solution)/shard_map/all_gather | solution.py:19
  8.0 67.9 %copy-start.4 = (bf16[2304,256]{1,0:T(8,128)(2,1)S(1)}, bf16[2304,256]{1,0:T(8,128)(2,1)}, u32[]{:S(2)}) copy-start(bf16[2304,256]{1,0:T(8,128)(2,1)} %param.9) | copy-start | bytes 3538948
  30.6 130.9 %reduce-scatter.2.cloned.1.call-start = ((), (), s32[]{:S(2)}) async-start(), calls=%async_computation.4 | async-start | bytes 7520256 | tf_op jit(solution)/shard_map/reduce_scatter | solution.py:55
  73.9 2.0 copy-start.1
  75.9 1.2 copy-start.5
  75.9 1.2 copy-start.6
  77.2 3.0 %copy-start.3 = (f32[256,256]{0,1:T(8,128)}, f32[256,256]{0,1:T(8,128)S(1)}, u32[]{:S(2)}) copy-start(f32[256,256]{0,1:T(8,128)S(1)} %fusion.5) | copy-start | bytes 786436
  142.2 36.2 %copy-start.2 = (bf16[2,256,2304]{2,1,0:T(8,128)(2,1)S(1)}, bf16[2,256,2304]{2,1,0:T(8,128)(2,1)}, u32[]{:S(2)}) copy-start(bf16[2,256,2304]{2,1,0:T(8,128)(2,1)} %all-gather.2.cloned.1.call-done) | copy-start | bytes 7077892
  166.7 29.3 %all-to-all-start.1 = ((f32[32,3,16,72]{3,2,1,0:T(8,128)}), f32[32,3,16,72]{3,2,1,0:T(8,128)}, u32[]{:S(2)}, u32[]{:S(2)}) async-start(f32[32,3,16,72]{3,2,1,0:T(8,128)} %bitcast.66), calls=%async_computation.2 | async-start | bytes 1572864 | tf_op jit(solution)/shard_map/all_to_all | solution.py:59
  178.4 18.8 %copy-start.7 = (f32[16]{0:T(128)S(1)}, f32[16]{0:T(128)}, u32[]{:S(2)}) copy-start(f32[16]{0:T(128)} %get-tuple-element.20) | copy-start | bytes 196
Sparse Core Ops, SparseCore 0:
  30.7 43.1 all-gather.1
  91.5 69.9 reduce-scatter.1
where the time goes:
time: 205 us
  waiting for transfers between devices  77.8 us (38%)
  blocking collectives  72.2 us (35%)
  between operations  14.2 us (7%)
  matrix products  12.1 us (6%)
  other arithmetic  12 us (6%)
  starting transfers between devices  9.91 us (5%)
  local copies, waits for them, and re-layouts  6.41 us (3%)
    psum x3, blocking collectives, local(): stats = lax.psum(lax.psum(lax.psum(local_stats, 'tok'), 'vy'), 'vx')  50.8 us
    all_gather x1, waiting for transfers between devices, local(): gathered = lax.all_gather(features, 'tok', axis=1, tiled=True)  43.2 us
    all_to_all x1, blocking collectives, local(): blocks = lax.all_to_all(copies, ('vy', 'vx'), 0, 0, tiled=True)  21.4 us
    reduce_scatter x1, waiting for transfers between devices, local(): summed = lax.psum_scatter(partials, 'tok', scatter_dimension=1, tiled=True)  19.3 us
    all_to_all x1, waiting for transfers between devices, local(): lax.all_to_all(blocks, ('vy', 'vx'), 0, 0, tiled=True)  15.3 us
    all_to_all x1, starting transfers between devices, local(): lax.all_to_all(blocks, ('vy', 'vx'), 0, 0, tiled=True)  9.83 us
    reshape x2, local copies, waits for them, and re-layouts, local(): summed.reshape(kinds, rows, voc_count, width // voc_count)  5.19 us
    another operation x1, other arithmetic, local(): jnp.stack([by_probe[0] + by_head[0], by_head[1], by_probe[1] + by_head[2]])  5.14 us
  transfers between devices with their start and end apart: 3, of which 3 were waited for; matrix products, arithmetic and copies ran while one was open for 2% of the time, Pallas kernels for 0%

commit v1 on v0

--- a/solution.py
+++ b/solution.py
@@ -16,7 +16,10 @@
     copies = jnp.broadcast_to(stacked[None], (voc_count,) + stacked.shape)
     blocks = lax.all_to_all(copies, ("vy", "vx"), 0, 0, tiled=True)
     features = blocks.transpose(1, 2, 0, 3).reshape(2, rows_here, voc_count * stacked.shape[2])
-    gathered = lax.all_gather(features, "tok", axis=1, tiled=True)
+    size = lax.axis_size("tok")
+    pieces = jnp.stack([features for _ in range(size)])
+    pieces = lax.all_to_all(pieces, "tok", split_axis=0, concat_axis=0)
+    gathered = jnp.concatenate(pieces, axis=1)
     row_hidden = gathered[0]
     row_probe = gathered[1]
     logits = jnp.dot(row_hidden, head, preferred_element_type=jnp.float32)

time: 205 us -> 227 us (1.11)
  starting transfers between devices: 9.91 us -> 20.4 us
  waiting for transfers between devices: 77.8 us -> 88 us
  local copies, waits for them, and re-layouts: 6.41 us -> 9.88 us
    all_to_all x0 -> x1, waiting for transfers between devices: none -> 54.9 us  [local(): pieces = lax.all_to_all(pieces, 'tok', split_axis=0, concat_axis=0)]
    all_gather x1 -> x0, waiting for transfers between devices: 43.2 us -> none  [local(): gathered = lax.all_gather(features, 'tok', axis=1, tiled=True)]
    all_to_all x0 -> x1, starting transfers between devices: none -> 10.5 us  [local(): pieces = lax.all_to_all(pieces, 'tok', split_axis=0, concat_axis=0)]
where the time goes in v1:
time: 227 us
  waiting for transfers between devices  88 us (39%)
  blocking collectives  70.4 us (31%)
  starting transfers between devices  20.4 us (9%)
  between operations  14.2 us (6%)
  other arithmetic  12.9 us (6%)
  matrix products  10.7 us (5%)
  local copies, waits for them, and re-layouts  9.88 us (4%)
    all_to_all x1, waiting for transfers between devices, local(): pieces = lax.all_to_all(pieces, 'tok', split_axis=0, concat_axis=0)  54.9 us
    psum x3, blocking collectives, local(): stats = lax.psum(lax.psum(lax.psum(local_stats, 'tok'), 'vy'), 'vx')  49.1 us
    all_to_all x1, blocking collectives, local(): blocks = lax.all_to_all(copies, ('vy', 'vx'), 0, 0, tiled=True)  21.3 us
    reduce_scatter x1, waiting for transfers between devices, local(): summed = lax.psum_scatter(partials, 'tok', scatter_dimension=1, tiled=True)  17.1 us
    all_to_all x1, waiting for transfers between devices, local(): lax.all_to_all(blocks, ('vy', 'vx'), 0, 0, tiled=True)  15.9 us
    all_to_all x1, starting transfers between devices, local(): pieces = lax.all_to_all(pieces, 'tok', split_axis=0, concat_axis=0)  10.5 us
    all_to_all x1, starting transfers between devices, local(): lax.all_to_all(blocks, ('vy', 'vx'), 0, 0, tiled=True)  9.93 us
    another operation x1, other arithmetic, local(): jnp.stack([by_probe[0] + by_head[0], by_head[1], by_probe[1] + by_head[2]])  5.74 us
  transfers between devices with their start and end apart: 3, of which 3 were waited for; matrix products, arithmetic and copies ran while one was open for 2% of the time, Pallas kernels for 0%

profile of v1, /device:TPU:2, one launch (start us, length us, event | category | flops | bytes accessed | tf_op | source)
XLA Modules:
  0.0 226.6 jit_solution(7275496071067780263)
XLA Ops:
  7.2 0.8 pad_maximum_fusion.1
  8.0 21.3 %all_to_all.15 = bf16[32,2,16,72]{3,2,1,0:T(8,128)(2,1)S(1)} all-to-all(bf16[32,2,16,72]{3,2,1,0:T(8,128)(2,1)S(1)} %broadcast_in_dim.2), channel_id=1, replica_groups=mesh['tok'=16,'vy'=8,'vx'=4] {'vy','vx'}, dimensions={0} | all-to-all | bytes 294912 | tf_op jit(solution)/shard_map/all_to_all | solution.py:17
  29.3 0.1 copy.21
  29.4 0.4 stack_reshape.2
  29.7 1.6 stack.57
  31.4 10.5 %all-to-all-start.1 = ((bf16[16,2,16,2304]{3,2,1,0:T(8,128)(2,1)}), bf16[16,2,16,2304]{3,2,1,0:T(8,128)(2,1)}, u32[]{:S(2)}, u32[]{:S(2)}) async-start(bf16[16,2,16,2304]{3,2,1,0:T(8,128)(2,1)} %stack.57), calls=%async_computation.1 | async-start | bytes 4718592 | tf_op jit(solution)/shard_map/all_to_all | solution.py:21
  41.9 0.0 reduce-scatter.2.cloned.1.call-start
  41.9 54.9 %all-to-all-done.1 = bf16[16,2,16,2304]{3,2,1,0:T(8,128)(2,1)} async-done(((bf16[16,2,16,2304]{3,2,1,0:T(8,128)(2,1)}), bf16[16,2,16,2304]{3,2,1,0:T(8,128)(2,1)}, u32[]{:S(2)}, u32[]{:S(2)}) %all-to-all-start.1) | async-done | bytes 2359328 | tf_op jit(solution)/shard_map/all_to_all | solution.py:21
  96.9 1.8 copy.36
  98.7 0.2 fusion.31
  98.9 0.6 fusion.33
  99.5 0.6 fusion.4
  100.2 0.6 convolution_add_fusion
  100.8 0.2 fusion.21
  101.0 0.5 copy-done.3
  101.5 2.7 %fusion.2 = f32[2,256,2304]{2,1,0:T(8,128)S(1)} fusion(bf16[2304,256]{1,0:T(8,128)(2,1)S(1)} %copy-done.1, f32[1,256,256]{1,2,0:T(8,128)S(1)} %get-tuple-element.21, f32[1,256,256]{1,2,0:T(8,128)S(1)} %get-tuple-element.22), kind=kOutput, calls=%fused_computation.6 | convolution fusion | flops 1812070400 | bytes 6422528 | tf_op jit(solution)/shard_map/dot_general | solution.py:41
  104.2 4.0 %fusion = f32[3,256,2304]{2,1,0:T(8,128)S(1)} fusion(bf16[2304,256]{1,0:T(8,128)(2,1)S(1)} %copy-done, f32[1,256,256]{1,2,0:T(8,128)S(1)} %get-tuple-element.18, f32[1,256,256]{1,2,0:T(8,128)S(1)} %get-tuple-element.22, f32[1,256,256]{1,2,0:T(8,128)S(1)} %get-tuple-element.17), kind=kOutput, calls=%fused_computation.4 | convolution fusion | flops 2718302208 | bytes 9043968 | tf_op jit(solution)/shard_map/dot_general | solution.py:48
  108.2 3.0 %slice_add_fusion.1 = (f32[1,256,2304]{2,1,0:T(8,128)S(1)}, f32[1,256,2304]{2,1,0:T(8,128)}, f32[1,256,2304]{2,1,0:T(8,128)}) fusion(f32[3,256,2304]{2,1,0:T(8,128)S(1)} %fusion, f32[2,256,2304]{2,1,0:T(8,128)S(1)} %fusion.2), kind=kLoop, calls=%fused_computation.3 | loop fusion | flops 1179648 | bytes 18874368 | tf_op jit(solution)/shard_map/add | solution.py:55
  111.2 5.7 %pad_maximum_fusion = f32[3,256,2304]{2,1,0:T(8,128)} fusion(f32[1,256,2304]{2,1,0:T(8,128)} %get-tuple-element.11, f32[1,256,2304]{2,1,0:T(8,128)} %get-tuple-element.12, f32[1,256,2304]{2,1,0:T(8,128)S(1)} %get-tuple-element.10), kind=kLoop, calls=%fused_computation | loop fusion | flops 3538944 | bytes 14155776 | tf_op jit(solution)/shard_map/stack | solution.py:55
  116.9 24.1 %psum.21 = f32[2,256]{1,0:T(2,128)S(1)} all-reduce(f32[2,256]{1,0:T(2,128)S(1)} %pad_maximum_fusion.2), channel_id=1, replica_groups=mesh['tok'=16,'vy'=8,'vx'=4] {'tok'}, use_global_device_ids=true, to_apply=%region_2.0 | all-reduce | flops 512 | bytes 4096 | tf_op jit(solution)/shard_map/psum | solution.py:59
  141.0 15.5 %psum.22 = f32[2,256]{1,0:T(2,128)S(1)} all-reduce(f32[2,256]{1,0:T(2,128)S(1)} %psum.21), channel_id=1, replica_groups=mesh['tok'=16,'vy'=8,'vx'=4] {'vy'}, use_global_device_ids=true, to_apply=%region_3.0 | all-reduce | flops 512 | bytes 4096 | tf_op jit(solution)/shard_map/psum | solution.py:59
  156.5 9.5 %psum.23 = f32[2,256]{1,0:T(2,128)S(1)} all-reduce(f32[2,256]{1,0:T(2,128)S(1)} %psum.22), channel_id=1, replica_groups=mesh['tok'=16,'vy'=8,'vx'=4] {'vx'}, use_global_device_ids=true, to_apply=%region_4.0 | all-reduce | flops 512 | bytes 4096 | tf_op jit(solution)/shard_map/psum | solution.py:59
  166.1 17.1 %reduce-scatter.2.cloned.1.call-done = f32[3,16,2304]{2,1,0:T(8,128)} async-done(((f32[3,256,2304]{2,1,0:T(8,128)}), f32[3,16,2304]{2,1,0:T(8,128)}) %reduce-scatter.2.cloned.1.call-update) | async-done | bytes 442384 | tf_op jit(solution)/shard_map/reduce_scatter | solution.py:58
  183.2 2.7 %reshape.55 = f32[3,16,32,72]{3,2,1,0:T(8,128)} reshape(f32[3,16,2304]{2,1,0:T(8,128)} %reduce-scatter.2.cloned.1.call-done) | data formatting | bytes 884736 | tf_op jit(solution)/shard_map/reshape | solution.py:61
  185.9 2.5 %copy.35 = f32[3,16,32,72]{3,1,0,2:T(8,128)} copy(f32[3,16,32,72]{3,2,1,0:T(8,128)} %reshape.55) | data formatting | bytes 884736 | tf_op jit(solution)/shard_map/reshape | solution.py:61
  188.4 9.9 %all-to-all-start.2 = ((f32[32,3,16,72]{3,2,1,0:T(8,128)}), f32[32,3,16,72]{3,2,1,0:T(8,128)}, u32[]{:S(2)}, u32[]{:S(2)}) async-start(f32[32,3,16,72]{3,2,1,0:T(8,128)} %bitcast.72), calls=%async_computation.3 | async-start | bytes 1572864 | tf_op jit(solution)/shard_map/all_to_all | solution.py:62
  198.3 0.1 bitcast_divide_fusion.1
  198.4 1.2 fusion.23
  199.7 2.2 convolution_bitcast_fusion
  201.9 15.9 %all-to-all-done.2 = f32[32,3,16,72]{3,2,1,0:T(8,128)} async-done(((f32[32,3,16,72]{3,2,1,0:T(8,128)}), f32[32,3,16,72]{3,2,1,0:T(8,128)}, u32[]{:S(2)}, u32[]{:S(2)}) %all-to-all-start.2) | async-done | bytes 442400 | tf_op jit(solution)/shard_map/all_to_all | solution.py:62
  217.9 1.2 reduce_sum.29
  219.1 0.7 fusion.24
  (17 shorter events, 0.2 us)
Async XLA Ops:
  7.2 91.7 %copy-start = (bf16[2304,256]{1,0:T(8,128)(2,1)S(1)}, bf16[2304,256]{1,0:T(8,128)(2,1)}, u32[]{:S(2)}) copy-start(bf16[2304,256]{1,0:T(8,128)(2,1)} %param.6) | copy-start | bytes 3538948
  31.4 65.5 %all-to-all-start.1 = ((bf16[16,2,16,2304]{3,2,1,0:T(8,128)(2,1)}), bf16[16,2,16,2304]{3,2,1,0:T(8,128)(2,1)}, u32[]{:S(2)}, u32[]{:S(2)}) async-start(bf16[16,2,16,2304]{3,2,1,0:T(8,128)(2,1)} %stack.57), calls=%async_computation.1 | async-start | bytes 4718592 | tf_op jit(solution)/shard_map/all_to_all | solution.py:21
  41.9 141.3 %reduce-scatter.2.cloned.1.call-start = ((), (), s32[]{:S(2)}) async-start(), calls=%async_computation.4 | async-start | bytes 7520256 | tf_op jit(solution)/shard_map/reduce_scatter | solution.py:58
  41.9 58.8 %copy-start.5 = (s32[256]{0:T(256)}, s32[256]{0:T(256)S(1)}, u32[]{:S(2)}) copy-start(s32[256]{0:T(256)S(1)} %iota_add_fusion) | copy-start | bytes 3076
  98.9 1.3 copy-start.1
  99.5 1.3 copy-start.4
  100.2 0.8 copy-start.2
  100.8 0.7 copy-start.3
  188.4 29.5 %all-to-all-start.2 = ((f32[32,3,16,72]{3,2,1,0:T(8,128)}), f32[32,3,16,72]{3,2,1,0:T(8,128)}, u32[]{:S(2)}, u32[]{:S(2)}) async-start(f32[32,3,16,72]{3,2,1,0:T(8,128)} %bitcast.72), calls=%async_computation.3 | async-start | bytes 1572864 | tf_op jit(solution)/shard_map/all_to_all | solution.py:62
Sparse Core Ops, SparseCore 0:
  117.0 66.0 reduce-scatter.1
